TPU v7x, 256 devices: a whole 4x4x8 slice. The times are simulated.
256 devices in a mesh: span: 8 (over z), ha: 8 (over x, core), wa: 4 (over y).
Axes of the slice: x: 4, y: 4, z: 8, core: 2. Of those that a mesh axis runs over, the one named last changes fastest.
Arguments:
- queries: bfloat16 [8, 3, 32, 48, 768], P('span', None, 'ha', 'wa'), may hold values from -5 to 5
- cache_keys: bfloat16 [8, 3, 32, 48, 768], P('span', None, 'ha', 'wa'), may hold values from -5 to 5
- cache_values: bfloat16 [8, 3, 32, 48, 768], P('span', None, 'ha', 'wa'), may hold values from -16 to 16
- grad_attended: bfloat16 [8, 3, 32, 48, 768], P('span', None, 'ha', 'wa'), may hold values from -16 to 16
- radius: int32 [6], replicated, may hold values from 1 to 2, as said below
- frame_count: int32 [8], replicated, may hold values from 1 to 3, as said below
Outputs:
- attended: bfloat16 [8, 3, 32, 48, 768], P('span', None, 'ha', 'wa')
- grad_queries: bfloat16 [8, 3, 32, 48, 768], P('span', None, 'ha', 'wa')
- grad_keys: bfloat16 [8, 3, 32, 48, 768], P('span', None, 'ha', 'wa')
- grad_values: bfloat16 [8, 3, 32, 48, 768], P('span', None, 'ha', 'wa')
Inputs may be any that keep to these rules, and one draw needn't show every extreme that they name: Some head has radius 2 and some other head has radius 1. Frame slots of block c at or past frame_count[c] hold padding; some block has all 3 slots live.
All inputs are finite; a program needn't handle non-finite values.
Results may differ from a plain program's by a relative error of at most 0.02.
Values may be sent and summed in bfloat16 or wider, within the bound.
A program may use at most 128 MiB of HBM per device.

v0:
```python
import math
import jax
import jax.numpy as jnp
from jax import lax
from jax.sharding import PartitionSpec as P

RMAX = 2


def padded(block, sides, width):
    for axis, dim in sides:
        count = lax.axis_size(axis)
        forward = [(i, i + 1) for i in range(count - 1)]
        backward = [(target, source) for source, target in forward]
        low = lax.ppermute(
            lax.slice_in_dim(block, block.shape[dim] - width, None, axis=dim), axis, forward
        )
        high = lax.ppermute(lax.slice_in_dim(block, 0, width, axis=dim), axis, backward)
        block = jnp.concatenate([low, block, high], axis=dim)
    return block


def near_table(radius, tile_h, tile_w, margin, first_row, first_col, full_h, full_w):
    rows_local = jnp.arange(tile_h)
    rows_wide = jnp.arange(tile_h + 2 * margin) - margin
    cols_local = jnp.arange(tile_w)
    cols_wide = jnp.arange(tile_w + 2 * margin) - margin
    gap_rows = jnp.abs(rows_local[:, None] - rows_wide[None, :])
    gap_cols = jnp.abs(cols_local[:, None] - cols_wide[None, :])
    inside_rows = (first_row + rows_wide >= 0) & (first_row + rows_wide < full_h)
    inside_cols = (first_col + cols_wide >= 0) & (first_col + cols_wide < full_w)
    reach = jnp.maximum(gap_rows[:, None, :, None], gap_cols[None, :, None, :])
    inside = inside_rows[:, None] & inside_cols[None, :]
    within = (reach[None] <= radius[:, None, None, None, None]) & inside[None, None, None]
    return within.reshape(
        radius.shape[0], tile_h * tile_w, (tile_h + 2 * margin) * (tile_w + 2 * margin)
    )


def with_frames(spatial, frame_live):
    heads, rows, columns = spatial.shape
    frames = frame_live.shape[0]
    joined = spatial[:, None, :, None, :] & frame_live[None, None, None, :, None]
    joined = jnp.broadcast_to(joined, (heads, frames, rows, frames, columns))
    return joined.reshape(heads, frames * rows, frames * columns)


def live_frames(frame_count, block_id, frames):
    picked = jnp.arange(frame_count.shape[0]) == block_id
    count = jnp.sum(jnp.where(picked, frame_count, 0))
    return jnp.arange(frames) < count


def over_tiles(advance, carried, piece):
    block_ids = jnp.arange(piece.shape[0], dtype=jnp.int32)

    def inner(current, item):
        return (advance(current, item[0], item[1]), None)

    result, _ = lax.scan(inner, carried, (piece, block_ids))
    return result


def shards(queries, cache_keys, cache_values, grad_attended, radius, frame_count):
    frames, tile_h, tile_w, width = queries.shape[1:]
    heads = radius.shape[0]
    depth = width // heads
    margin = RMAX
    scale = 1.0 / math.sqrt(depth)
    own_block = lax.axis_index("span")
    block_total = lax.axis_size("span")
    first_row = lax.axis_index("ha") * tile_h
    first_col = lax.axis_index("wa") * tile_w
    spatial = near_table(
        radius,
        tile_h,
        tile_w,
        margin,
        first_row,
        first_col,
        tile_h * lax.axis_size("ha"),
        tile_w * lax.axis_size("wa"),
    )
    local_rows = frames * tile_h * tile_w
    wide_rows = frames * (tile_h + 2 * margin) * (tile_w + 2 * margin)
    query_rows = queries.reshape(local_rows, heads, depth)
    key_local = cache_keys.reshape(local_rows, heads, depth)
    value_local = cache_values.reshape(local_rows, heads, depth)
    upstream = grad_attended.reshape(local_rows, heads, depth)
    key_mask = with_frames(
        jnp.transpose(spatial, (0, 2, 1)), live_frames(frame_count, own_block, frames)
    )
    bundle = jnp.concatenate([cache_keys, cache_values, queries, grad_attended], axis=4)

    def forward_step(carried, tile, block_id):

        def forward_run(current):
            top, total, accum = current
            key_rows = tile[..., :width].reshape(wide_rows, heads, depth)
            value_rows = tile[..., width : 2 * width].reshape(wide_rows, heads, depth)
            allowed = with_frames(spatial, live_frames(frame_count, block_id, frames))
            score = (
                jnp.einsum("qhd,khd->hqk", query_rows, key_rows, preferred_element_type=jnp.float32)
                * scale
            )
            score = jnp.where(allowed, score, -jnp.inf)
            new_top = jnp.maximum(top, jnp.max(score, axis=2))
            weight = jnp.exp(score - new_top[:, :, None])
            fading = jnp.exp(top - new_top)
            total = total * fading + jnp.sum(weight, axis=2)
            accum = accum * fading[:, :, None] + jnp.einsum(
                "hqk,khd->hqd",
                weight.astype(jnp.bfloat16),
                value_rows,
                preferred_element_type=jnp.float32,
            )
            return (new_top, total, accum)

        active = (block_id >= 0) & (block_id <= own_block)
        return lax.cond(active, forward_run, lambda current: current, carried)

    def query_grad_step(carried, tile, block_id):

        def query_run(current):
            key_rows = tile[..., :width].reshape(wide_rows, heads, depth)
            value_rows = tile[..., width : 2 * width].reshape(wide_rows, heads, depth)
            allowed = with_frames(spatial, live_frames(frame_count, block_id, frames))
            score = (
                jnp.einsum("qhd,khd->hqk", query_rows, key_rows, preferred_element_type=jnp.float32)
                * scale
            )
            prob = jnp.exp(jnp.where(allowed, score - log_total[:, :, None], -jnp.inf))
            push = jnp.einsum(
                "qhd,khd->hqk", upstream, value_rows, preferred_element_type=jnp.float32
            )
            slope = (prob * (push - delta[:, :, None])).astype(jnp.bfloat16)
            return current + jnp.einsum(
                "hqk,khd->hqd", slope, key_rows, preferred_element_type=jnp.float32
            )

        active = (block_id >= 0) & (block_id <= own_block)
        return lax.cond(active, query_run, lambda current: current, carried)

    def key_grad_step(carried, tile, block_id):

        def key_run(current):
            grad_k, grad_v = current
            asking = tile[..., -2 * width : -width].reshape(wide_rows, heads, depth)
            asking_grad = tile[..., -width:].reshape(wide_rows, heads, depth)
            stat_tile = lax.dynamic_index_in_dim(
                stats_all, jnp.clip(block_id, 0, block_total - 1), 0, keepdims=False
            )
            stat_rows = stat_tile.reshape(wide_rows, 2 * heads)
            row_lse = jnp.transpose(stat_rows[:, :heads])
            row_delta = jnp.transpose(stat_rows[:, heads:])
            score = (
                jnp.einsum("qhd,khd->hqk", asking, key_local, preferred_element_type=jnp.float32)
                * scale
            )
            prob = jnp.exp(jnp.where(key_mask, score - row_lse[:, :, None], -jnp.inf))
            grad_v = grad_v + jnp.einsum(
                "hqk,qhd->khd",
                prob.astype(jnp.bfloat16),
                asking_grad,
                preferred_element_type=jnp.float32,
            )
            push = jnp.einsum(
                "qhd,khd->hqk", asking_grad, value_local, preferred_element_type=jnp.float32
            )
            slope = (prob * (push - row_delta[:, :, None])).astype(jnp.bfloat16)
            grad_k = grad_k + jnp.einsum(
                "hqk,qhd->khd", slope, asking, preferred_element_type=jnp.float32
            )
            return (grad_k, grad_v)

        active = (block_id >= own_block) & (block_id < block_total)
        return lax.cond(active, key_run, lambda current: current, carried)

    start_state = (
        jnp.full((heads, local_rows), -jnp.inf, jnp.float32),
        jnp.zeros((heads, local_rows), jnp.float32),
        jnp.zeros((heads, local_rows, depth), jnp.float32),
    )
    everything = lax.all_gather(bundle, "span", axis=0, tiled=True)
    wide_all = padded(everything, (("ha", 2), ("wa", 3)), RMAX)
    top, total, accum = over_tiles(forward_step, start_state, wide_all)
    attended_rows = jnp.transpose((accum / total[:, :, None]).astype(jnp.bfloat16), (1, 0, 2))
    log_total = top + jnp.log(total)
    delta = jnp.einsum("qhd,qhd->hq", upstream, attended_rows, preferred_element_type=jnp.float32)
    stats = jnp.concatenate([jnp.transpose(log_total), jnp.transpose(delta)], axis=1)
    stats = stats.reshape(1, frames, tile_h, tile_w, 2 * heads)
    stat_wide = padded(stats, (("ha", 2), ("wa", 3)), RMAX)
    stats_all = lax.all_gather(stat_wide, "span", axis=0, tiled=True)
    query_start = jnp.zeros((heads, local_rows, depth), jnp.float32)
    key_start = (
        jnp.zeros((local_rows, heads, depth), jnp.float32),
        jnp.zeros((local_rows, heads, depth), jnp.float32),
    )
    grad_q = over_tiles(query_grad_step, query_start, wide_all)
    grad_k, grad_v = over_tiles(key_grad_step, key_start, wide_all)
    final = (1, frames, tile_h, tile_w, width)
    attended = attended_rows.reshape(final)
    grad_queries = jnp.transpose(grad_q * scale, (1, 0, 2)).astype(jnp.bfloat16).reshape(final)
    grad_keys = (grad_k * scale).astype(jnp.bfloat16).reshape(final)
    grad_values = grad_v.astype(jnp.bfloat16).reshape(final)
    return (attended, grad_queries, grad_keys, grad_values)


def solution(mesh):
    placed = (
        P("span", None, "ha", "wa", None),
        P("span", None, "ha", "wa", None),
        P("span", None, "ha", "wa", None),
        P("span", None, "ha", "wa", None),
        P(),
        P(),
    )
    return jax.shard_map(
        shards,
        mesh=mesh,
        in_specs=placed,
        out_specs=(
            P("span", None, "ha", "wa", None),
            P("span", None, "ha", "wa", None),
            P("span", None, "ha", "wa", None),
            P("span", None, "ha", "wa", None),
        ),
        check_vma=False,
    )
```

profile of v0, /device:TPU:2, one launch (start us, length us, event | category | flops | bytes accessed | tf_op | source)
XLA Modules:
  0.0 646.9 jit_solution(17913290227682815183)
XLA Ops:
  9.8 84.9 %all-gather.2.cloned.1.call-done = bf16[8,3,4,12,3072]{4,2,3,1,0:T(4,128)(2,1)} async-done(((bf16[1,3,4,12,3072]{4,2,3,1,0:T(4,128)(2,1)}), bf16[8,3,4,12,3072]{4,2,3,1,0:T(4,128)(2,1)}) %all-gather.2.cloned.1.call-update) | async-done | bytes 7077904 | tf_op jit(solution)/shard_map/all_gather | solution.py:184
  94.7 9.5 %fusion.57 = (bf16[8,3,2,12,3072]{4,2,3,1,0:T(2,128)(2,1)S(1)}, bf16[8,3,2,12,3072]{4,2,3,1,0:T(2,128)(2,1)S(1)}) fusion(bf16[8,3,4,12,3072]{4,2,3,1,0:T(4,128)(2,1)} %all-gather.2.cloned.1.call-done), kind=kLoop, calls=%fused_computation.100 | loop fusion | bytes 14155776 | tf_op jit(solution)/shard_map/slice | solution.py:16
  116.3 32.7 %collective-permute-done = bf16[8,3,2,12,3072]{4,0,3,2,1:T(8,128)(2,1)S(1)} collective-permute-done((bf16[8,3,2,12,3072]{4,0,3,2,1:T(8,128)(2,1)S(1)}, bf16[8,3,2,12,3072]{4,0,3,2,1:T(8,128)(2,1)S(1)}, u32[]{:S(2)}, u32[]{:S(2)}) %collective-permute-start) | collective-permute-done | bytes 3538976 | tf_op jit(solution)/shard_map/ppermute | solution.py:15
  155.2 5.6 copy.88
  160.9 5.3 pad_maximum_fusion.3
  166.2 4.8 collective-permute-start.2
  198.0 22.7 %collective-permute-done.2 = bf16[8,3,8,2,3072]{4,2,3,1,0:T(8,128)(2,1)} collective-permute-done((bf16[8,3,8,2,3072]{4,2,3,1,0:T(8,128)(2,1)}, bf16[8,3,8,2,3072]{4,2,3,1,0:T(8,128)(2,1)}, u32[]{:S(2)}, u32[]{:S(2)}) %collective-permute-start.2) | collective-permute-done | bytes 2359328 | tf_op jit(solution)/shard_map/ppermute | solution.py:15
  220.7 6.0 collective-permute-done.3
  226.8 13.9 %pad_maximum_fusion = bf16[8,3,8,16,3072]{4,2,3,1,0:T(8,128)(2,1)S(1)} fusion(bf16[8,3,8,2,3072]{4,2,3,1,0:T(8,128)(2,1)} %collective-permute-done.3, bf16[8,3,2,12,3072]{4,2,3,1,0:T(2,128)(2,1)} %copy-done, bf16[8,3,4,12,3072]{4,2,3,1,0:T(4,128)(2,1)} %all-gather.2.cloned.1.call-done, bf16[8,3,2,12,3072]{4,2,3,1,0:T(2,128)(2,1)S(1)} %copy.87, ...), kind=kLoop, calls=%fused_computation.67 | loop fusion | flops 94371840 | bytes 37748736 | tf_op jit(solution)/shard_map/concatenate | solution.py:19
  240.7 12.6 %copy.90 = bf16[8,3,8,16,3072]{4,3,2,1,0:T(8,128)(2,1)} copy(bf16[8,3,8,16,3072]{4,2,3,1,0:T(8,128)(2,1)S(1)} %pad_maximum_fusion) | data formatting | bytes 37748736
  253.4 26.6 %while.42 = (s32[]{:T(128)}, f32[6,144]{1,0:T(8,128)S(1)}, f32[6,144]{1,0:T(8,128)S(1)}, f32[6,144,128]{2,1,0:T(8,128)S(1)}, s32[8]{0:T(128)S(1)}, /*index=5*/s3...) while((s32[]{:T(128)}, f32[6,144]{1,0:T(8,128)S(1)}, ...), condition=%wide.region_6.7_spmd.clone, body=%wide.region_0.6_spmd.clone.sunk | while | flops 172599008 | bytes 17480200 | solution.py:60
  255.3 11.1 %conditional.9 = ((f32[6,144]{1,0:T(8,128)S(1)}, f32[6,144]{1,0:T(8,128)S(1)}, f32[6,144,128]{2,1,0:T(8,128)S(1)})) conditional(s32[]{:T(128)} %convert_element_type.76, (f32[6,144]{1,0:T(8,128)S(1)}, f32[6,144]{1,0:T(8,128)S(1)}, f32[6,144,128]{2,1,0:T(8,128)S(1)}) %tuple.115, (s32[4,12,8,16]{3,2,1,0:T(8,128)S(1)}, s32[]{:T(128)}, s32[8]{0:T(128)}, ...), branch_computations={%region_1.1_spmd, %region_2.0_spmd} | conditional | flops 172599008 | bytes 17479918 | solution.py:120
  290.0 29.6 %while.43 = (s32[]{:T(128)}, f32[6,144,128]{2,1,0:T(8,128)}, s32[8]{0:T(128)}, s32[]{:T(128)}, s32[8]{0:T(128)}, /*index=5*/bf16[8,3,8,16,3072]{4,3,2,1,0:T(8,12...) while((s32[]{:T(128)}, f32[6,144,128]{2,1,0:T(8,128)}, ...), condition=%wide.region_11.12_spmd.clone, body=%wide.region_7.11_spmd.clone.sunk | while | flops 257089568 | bytes 18095392 | solution.py:60
  292.3 11.0 %conditional.10 = (f32[6,144,128]{2,1,0:T(8,128)}) conditional(s32[]{:T(128)} %convert_element_type.77, f32[6,144,128]{2,1,0:T(8,128)} %get-tuple-element.945, (s32[4,12,8,16]{3,2,1,0:T(8,128)S(1)}, s32[]{:T(128)}, s32[8]{0:T(128)}, bf16[8,3,8,16,3072]{4,3,2,1,0:T(8,128)(2,1)}, s32[]{:T(128)}, /*index=5*/bf16[144,6,128]{2,0,1:T(8,128)(2,1)}, ...), branch_computations={%region_8.8_spmd, %region_9.10_spmd} | conditional | flops 257089568 | bytes 18095118 | solution.py:142
  331.2 180.3 %all_gather.7 = f32[8,3,8,16,12]{3,2,4,1,0:T(8,128)S(1)} all-gather(f32[1,3,8,16,12]{3,2,4,1,0:T(8,128)S(1)} %copy.99), channel_id=1, replica_groups=mesh['span'=8,'ha'=8,'wa'=4] {'span'}, dimensions={0}, use_global_device_ids=true | all-gather | bytes 165888 | tf_op jit(solution)/shard_map/all_gather | solution.py:193
  513.5 122.9 %while.44 = (s32[]{:T(128)}, f32[144,6,128]{2,0,1:T(8,128)S(1)}, f32[144,6,128]{2,0,1:T(8,128)}, s32[8]{0:T(128)S(1)}, s32[]{:T(128)}, /*index=5*/bf16[8,3,8,16,...) while((s32[]{:T(128)}, f32[144,6,128]{2,0,1:T(8,128)S(1)}, ...), condition=%wide.region_16.17_spmd.clone, body=%wide.region_13.16_spmd.clone.sunk | while | flops 342282240 | bytes 23095652 | solution.py:60
  515.4 13.5 %conditional.11 = ((f32[144,6,128]{2,0,1:T(8,128)S(1)}, f32[144,6,128]{2,0,1:T(8,128)})) conditional(s32[]{:T(128)} %convert_element_type.78, (f32[144,6,128]{2,0,1:T(8,128)S(1)}, f32[144,6,128]{2,0,1:T(8,128)}) %tuple.120, (bf16[8,3,8,16,3072]{4,3,2,1,0:T(8,128)(2,1)}, s32[]{:T(128)}, bf16[144,6,128]{2,0,1:T(8,128)(2,1)}, s32[]{:T(128)}, ...), branch_computations={%region_14.14_spmd, %region_15.15_spmd} | conditional | flops 342282240 | bytes 23095408 | solution.py:177
  530.8 13.5 %conditional.11 = ((f32[144,6,128]{2,0,1:T(8,128)S(1)}, f32[144,6,128]{2,0,1:T(8,128)})) conditional(s32[]{:T(128)} %convert_element_type.78, (f32[144,6,128]{2,0,1:T(8,128)S(1)}, f32[144,6,128]{2,0,1:T(8,128)}) %tuple.120, (bf16[8,3,8,16,3072]{4,3,2,1,0:T(8,128)(2,1)}, s32[]{:T(128)}, bf16[144,6,128]{2,0,1:T(8,128)(2,1)}, s32[]{:T(128)}, ...), branch_computations={%region_14.14_spmd, %region_15.15_spmd} | conditional | flops 342282240 | bytes 23095408 | solution.py:177
  546.1 13.5 %conditional.11 = ((f32[144,6,128]{2,0,1:T(8,128)S(1)}, f32[144,6,128]{2,0,1:T(8,128)})) conditional(s32[]{:T(128)} %convert_element_type.78, (f32[144,6,128]{2,0,1:T(8,128)S(1)}, f32[144,6,128]{2,0,1:T(8,128)}) %tuple.120, (bf16[8,3,8,16,3072]{4,3,2,1,0:T(8,128)(2,1)}, s32[]{:T(128)}, bf16[144,6,128]{2,0,1:T(8,128)(2,1)}, s32[]{:T(128)}, ...), branch_computations={%region_14.14_spmd, %region_15.15_spmd} | conditional | flops 342282240 | bytes 23095408 | solution.py:177
  561.5 13.5 %conditional.11 = ((f32[144,6,128]{2,0,1:T(8,128)S(1)}, f32[144,6,128]{2,0,1:T(8,128)})) conditional(s32[]{:T(128)} %convert_element_type.78, (f32[144,6,128]{2,0,1:T(8,128)S(1)}, f32[144,6,128]{2,0,1:T(8,128)}) %tuple.120, (bf16[8,3,8,16,3072]{4,3,2,1,0:T(8,128)(2,1)}, s32[]{:T(128)}, bf16[144,6,128]{2,0,1:T(8,128)(2,1)}, s32[]{:T(128)}, ...), branch_computations={%region_14.14_spmd, %region_15.15_spmd} | conditional | flops 342282240 | bytes 23095408 | solution.py:177
  576.9 13.5 %conditional.11 = ((f32[144,6,128]{2,0,1:T(8,128)S(1)}, f32[144,6,128]{2,0,1:T(8,128)})) conditional(s32[]{:T(128)} %convert_element_type.78, (f32[144,6,128]{2,0,1:T(8,128)S(1)}, f32[144,6,128]{2,0,1:T(8,128)}) %tuple.120, (bf16[8,3,8,16,3072]{4,3,2,1,0:T(8,128)(2,1)}, s32[]{:T(128)}, bf16[144,6,128]{2,0,1:T(8,128)(2,1)}, s32[]{:T(128)}, ...), branch_computations={%region_14.14_spmd, %region_15.15_spmd} | conditional | flops 342282240 | bytes 23095408 | solution.py:177
  592.2 13.5 %conditional.11 = ((f32[144,6,128]{2,0,1:T(8,128)S(1)}, f32[144,6,128]{2,0,1:T(8,128)})) conditional(s32[]{:T(128)} %convert_element_type.78, (f32[144,6,128]{2,0,1:T(8,128)S(1)}, f32[144,6,128]{2,0,1:T(8,128)}) %tuple.120, (bf16[8,3,8,16,3072]{4,3,2,1,0:T(8,128)(2,1)}, s32[]{:T(128)}, bf16[144,6,128]{2,0,1:T(8,128)(2,1)}, s32[]{:T(128)}, ...), branch_computations={%region_14.14_spmd, %region_15.15_spmd} | conditional | flops 342282240 | bytes 23095408 | solution.py:177
  607.6 13.5 %conditional.11 = ((f32[144,6,128]{2,0,1:T(8,128)S(1)}, f32[144,6,128]{2,0,1:T(8,128)})) conditional(s32[]{:T(128)} %convert_element_type.78, (f32[144,6,128]{2,0,1:T(8,128)S(1)}, f32[144,6,128]{2,0,1:T(8,128)}) %tuple.120, (bf16[8,3,8,16,3072]{4,3,2,1,0:T(8,128)(2,1)}, s32[]{:T(128)}, bf16[144,6,128]{2,0,1:T(8,128)(2,1)}, s32[]{:T(128)}, ...), branch_computations={%region_14.14_spmd, %region_15.15_spmd} | conditional | flops 342282240 | bytes 23095408 | solution.py:177
  622.9 13.5 %conditional.11 = ((f32[144,6,128]{2,0,1:T(8,128)S(1)}, f32[144,6,128]{2,0,1:T(8,128)})) conditional(s32[]{:T(128)} %convert_element_type.78, (f32[144,6,128]{2,0,1:T(8,128)S(1)}, f32[144,6,128]{2,0,1:T(8,128)}) %tuple.120, (bf16[8,3,8,16,3072]{4,3,2,1,0:T(8,128)(2,1)}, s32[]{:T(128)}, bf16[144,6,128]{2,0,1:T(8,128)(2,1)}, s32[]{:T(128)}, ...), branch_computations={%region_14.14_spmd, %region_15.15_spmd} | conditional | flops 342282240 | bytes 23095408 | solution.py:177
  (307 shorter events, 217.4 us)
Async XLA Ops:
  7.2 87.6 %all-gather.2.cloned.1.call-start = ((), (), s32[]{:S(2)}) async-start(), calls=%async_computation | async-start | bytes 7962624 | tf_op jit(solution)/shard_map/all_gather | solution.py:184
  106.2 42.8 %collective-permute-start = (bf16[8,3,2,12,3072]{4,0,3,2,1:T(8,128)(2,1)S(1)}, bf16[8,3,2,12,3072]{4,0,3,2,1:T(8,128)(2,1)S(1)}, u32[]{:S(2)}, u32[]{:S(2)}) collective-permute-start(bf16[8,3,2,12,3072]{4,0,3,2,1:T(8,128)(2,1)S(1)} %copy.85), channel_id=1, source_target_pairs={{0,4},{4,8},{8,12},{12,16},{16,20},{20,24},{24,28},{1,5},{5,9},{9,... | collective-permute-start | bytes 10616840 | tf_op jit(solution)/shard_map/ppermute | solution.py:15
  108.1 52.7 %slice-start = ((s8[7077888]{0:T(1024)(128)(4,1)}), s8[4194304]{0:T(1024)(128)(4,1)S(1)}, s32[]{:S(2)}) async-start(s8[7077888]{0:T(1024)(128)(4,1)} %bitcast.91), calls=%async_computation.1 | async-start | bytes 8388608
  112.0 48.9 %slice-start.1 = ((s8[7077888]{0:T(1024)(128)(4,1)}), s8[2883584]{0:T(1024)(128)(4,1)S(1)}, s32[]{:S(2)}) async-start(s8[7077888]{0:T(1024)(128)(4,1)} %bitcast.91), calls=%async_computation.2 | async-start | bytes 5767168
  112.0 43.2 %collective-permute-start.1 = (bf16[8,3,2,12,3072]{4,0,3,2,1:T(8,128)(2,1)}, bf16[8,3,2,12,3072]{4,0,3,2,1:T(8,128)(2,1)}, u32[]{:S(2)}, u32[]{:S(2)}) collective-permute-start(bf16[8,3,2,12,3072]{4,0,3,2,1:T(8,128)(2,1)} %copy.86), channel_id=1, source_target_pairs={{4,0},{8,4},{12,8},{16,12},{20,16},{24,20},{28,24},{5,1},{9,5},{13... | collective-permute-start | bytes 10616840 | tf_op jit(solution)/shard_map/ppermute | solution.py:18
  160.8 5.3 copy-start
  160.8 11.6 %copy-start.5 = (bf16[1,3,4,12,768]{4,2,3,1,0:T(4,128)(2,1)S(1)}, bf16[1,3,4,12,768]{4,2,3,1,0:T(4,128)(2,1)}, u32[]{:S(2)}) copy-start(bf16[1,3,4,12,768]{4,2,3,1,0:T(4,128)(2,1)} %param.18) | copy-start | bytes 663556
  160.9 12.3 %copy-start.6 = (bf16[1,3,4,12,768]{4,2,3,1,0:T(4,128)(2,1)S(1)}, bf16[1,3,4,12,768]{4,2,3,1,0:T(4,128)(2,1)}, u32[]{:S(2)}) copy-start(bf16[1,3,4,12,768]{4,2,3,1,0:T(4,128)(2,1)} %param.21) | copy-start | bytes 663556
  160.9 13.0 %copy-start.7 = (bf16[1,3,4,12,768]{4,2,3,1,0:T(4,128)(2,1)S(1)}, bf16[1,3,4,12,768]{4,2,3,1,0:T(4,128)(2,1)}, u32[]{:S(2)}) copy-start(bf16[1,3,4,12,768]{4,2,3,1,0:T(4,128)(2,1)} %param.19) | copy-start | bytes 663556
  160.9 13.8 %copy-start.8 = (bf16[1,3,4,12,768]{4,2,3,1,0:T(4,128)(2,1)S(1)}, bf16[1,3,4,12,768]{4,2,3,1,0:T(4,128)(2,1)}, u32[]{:S(2)}) copy-start(bf16[1,3,4,12,768]{4,2,3,1,0:T(4,128)(2,1)} %param.20) | copy-start | bytes 663556
  166.2 54.5 %collective-permute-start.2 = (bf16[8,3,8,2,3072]{4,2,3,1,0:T(8,128)(2,1)}, bf16[8,3,8,2,3072]{4,2,3,1,0:T(8,128)(2,1)}, u32[]{:S(2)}, u32[]{:S(2)}) collective-permute-start(bf16[8,3,8,2,3072]{4,2,3,1,0:T(8,128)(2,1)} %get-tuple-element.644), channel_id=1, source_target_pairs={{0,1},{1,2},{2,3},{4,5},{5,6},{6,7},{8,9},{9,10},{10,11},{12,13},{... | collective-permute-start | bytes 7077896 | tf_op jit(solution)/shard_map/ppermute | solution.py:15
  170.9 55.8 %collective-permute-start.3 = (bf16[8,3,8,2,3072]{4,2,3,1,0:T(8,128)(2,1)}, bf16[8,3,8,2,3072]{4,2,3,1,0:T(8,128)(2,1)}, u32[]{:S(2)}, u32[]{:S(2)}) collective-permute-start(bf16[8,3,8,2,3072]{4,2,3,1,0:T(8,128)(2,1)} %get-tuple-element.645), channel_id=1, source_target_pairs={{1,0},{2,1},{3,2},{5,4},{6,5},{7,6},{9,8},{10,9},{11,10},{13,12},{... | collective-permute-start | bytes 7077896 | tf_op jit(solution)/shard_map/ppermute | solution.py:18
  175.4 21.0 %copy-start.11 = (s32[6]{0:T(128)S(1)}, s32[6]{0:T(128)}, u32[]{:S(2)}) copy-start(s32[6]{0:T(128)} %param.22) | copy-start | bytes 76
  183.2 10.6 %copy-start.12 = (pred[128]{0:T(512)(128)(4,1)S(1)}, pred[128]{0:T(512)(128)(4,1)}, u32[]{:S(2)}) copy-start(pred[128]{0:T(512)(128)(4,1)} %and.135) | copy-start | bytes 388
  240.7 12.7 %copy-start.1 = (s32[4,12,8,16]{3,2,1,0:T(8,128)S(1)}, s32[4,12,8,16]{3,2,1,0:T(8,128)}, u32[]{:S(2)}) copy-start(s32[4,12,8,16]{3,2,1,0:T(8,128)} %broadcast_maximum_fusion) | copy-start | bytes 73732
  282.9 36.7 %collective-permute-start.4 = (f32[1,3,2,12,12]{3,2,1,4,0:T(2,128)}, f32[1,3,2,12,12]{3,2,1,4,0:T(2,128)}, u32[]{:S(2)}, u32[]{:S(2)}) collective-permute-start(f32[1,3,2,12,12]{3,2,1,4,0:T(2,128)} %get-tuple-element.652), channel_id=1, source_target_pairs={{0,4},{4,8},{8,12},{12,16},{16,20},{20,24},{24,28},{1,5},{5,9},{9,... | collective-permute-start | bytes 10376 | tf_op jit(solution)/shard_map/ppermute | solution.py:15
  285.1 34.5 %collective-permute-start.5 = (f32[1,3,2,12,12]{3,2,1,4,0:T(2,128)}, f32[1,3,2,12,12]{3,2,1,4,0:T(2,128)}, u32[]{:S(2)}, u32[]{:S(2)}) collective-permute-start(f32[1,3,2,12,12]{3,2,1,4,0:T(2,128)} %get-tuple-element.653), channel_id=1, source_target_pairs={{4,0},{8,4},{12,8},{16,12},{20,16},{24,20},{28,24},{5,1},{9,5},{13... | collective-permute-start | bytes 10376 | tf_op jit(solution)/shard_map/ppermute | solution.py:18
  295.5 5.1 copy-start.10
  319.6 6.6 %copy-start.9 = (bf16[144,6,128]{2,0,1:T(8,128)(2,1)S(1)}, bf16[144,6,128]{2,0,1:T(8,128)(2,1)}, u32[]{:S(2)}) copy-start(bf16[144,6,128]{2,0,1:T(8,128)(2,1)} %get-tuple-element.649) | copy-start | bytes 663556
  320.7 6.7 %collective-permute-start.6 = (f32[1,3,8,2,12]{3,2,1,4,0:T(8,128)S(1)}, f32[1,3,8,2,12]{3,2,1,4,0:T(8,128)S(1)}, u32[]{:S(2)}, u32[]{:S(2)}) collective-permute-start(f32[1,3,8,2,12]{3,2,1,4,0:T(8,128)S(1)} %get-tuple-element.650), channel_id=1, source_target_pairs={{0,1},{1,2},{2,3},{4,5},{5,6},{6,7},{8,9},{9,10},{10,11},{12,13},{... | collective-permute-start | bytes 6920 | tf_op jit(solution)/shard_map/ppermute | solution.py:15
  322.7 7.5 %collective-permute-start.7 = (f32[1,3,8,2,12]{3,2,1,4,0:T(8,128)S(1)}, f32[1,3,8,2,12]{3,2,1,4,0:T(8,128)S(1)}, u32[]{:S(2)}, u32[]{:S(2)}) collective-permute-start(f32[1,3,8,2,12]{3,2,1,4,0:T(8,128)S(1)} %get-tuple-element.651), channel_id=1, source_target_pairs={{1,0},{2,1},{3,2},{5,4},{6,5},{7,6},{9,8},{10,9},{11,10},{13,12},{... | collective-permute-start | bytes 6920 | tf_op jit(solution)/shard_map/ppermute | solution.py:18
  542.0 2.2 copy-start.3
  572.7 2.2 copy-start.3
  603.5 2.2 copy-start.3
  (14 other events, 28.3 us)
Sparse Core Ops, SparseCore 0:
  10.0 84.7 all-gather.1
where the time goes:
time: 655 us; the launch traced here: 647 us
  blocking collectives  180 us (27%)
  waiting for transfers between devices  152 us (23%)
  local copies, waits for them, and re-layouts  147 us (22%)
  matrix products  55.1 us (8%)
  other arithmetic  39.6 us (6%)
  loops' own time  36.7 us (6%)
  starting transfers between devices  21.6 us (3%)
  between operations  14.7 us (2%)
    all_gather x1, blocking collectives, shards(): stats_all = lax.all_gather(stat_wide, 'span', axis=0, tiled=True)  180 us
    all_gather x1, waiting for transfers between devices, shards(): everything = lax.all_gather(bundle, 'span', axis=0, tiled=True)  84.9 us
    ppermute x4, waiting for transfers between devices, padded(): lax.ppermute(lax.slice_in_dim(block, block.shape[dim] - width, None, axis...  55.4 us
    another operation x3, loops' own time, over_tiles(): result, _ = lax.scan(inner, carried, (piece, block_ids))  30.3 us
    unnamed x36, local copies, waits for them, and re-layouts  26.6 us
    dot_general x8, matrix products, key_run(): jnp.einsum('hqk,qhd->khd', slope, asking, preferred_element_type=jnp.floa...  20.5 us
    squeeze x10, local copies, waits for them, and re-layouts, over_tiles(): result, _ = lax.scan(inner, carried, (piece, block_ids))  19.7 us
    dynamic_slice x24, local copies, waits for them, and re-layouts, over_tiles(): result, _ = lax.scan(inner, carried, (piece, block_ids))  18.6 us
  transfers between devices with their start and end apart: 9, of which 6 were waited for; matrix products, arithmetic and copies ran while one was open for 9% of the time, Pallas kernels for 0%

commit v1 on v0

--- a/solution.py
+++ b/solution.py
@@ -181,7 +181,16 @@
         jnp.zeros((heads, local_rows), jnp.float32),
         jnp.zeros((heads, local_rows, depth), jnp.float32),
     )
-    everything = lax.all_gather(bundle, "span", axis=0, tiled=True)
+    skins_assign = lambda local_values: jnp.concatenate(
+        jax.lax.all_to_all(
+            jnp.stack([local_values for _ in range(jax.lax.axis_size("span"))], axis=0),
+            axis_name="span",
+            split_axis=0,
+            concat_axis=0,
+        ),
+        0,
+    )
+    everything = skins_assign(bundle)
     wide_all = padded(everything, (("ha", 2), ("wa", 3)), RMAX)
     top, total, accum = over_tiles(forward_step, start_state, wide_all)
     attended_rows = jnp.transpose((accum / total[:, :, None]).astype(jnp.bfloat16), (1, 0, 2))

time: 655 us -> 723 us (1.10)
  blocking collectives: 180 us -> 344 us
  waiting for transfers between devices: 152 us -> 66.8 us
  between operations: 14.7 us -> 1.24 us
    all_to_all x0 -> x1, blocking collectives: none -> 166 us  [shards(): jax.lax.all_to_all(jnp.stack([local_values for _ in range(jax.lax.axis_si...]
    all_gather x1 -> x0, waiting for transfers between devices: 84.9 us -> none  [shards(): everything = lax.all_gather(bundle, 'span', axis=0, tiled=True)]
    unnamed x36 -> x34, local copies, waits for them, and re-layouts: 26.6 us -> 26.6 us
  transfers between devices with their start and end apart: 9 -> 8, of which waited for: 6 -> 5; matrix products, arithmetic and copies ran while one was open for 9% -> 8% of each run, Pallas kernels for 0% -> 0%
where the time goes in v1:
time: 723 us; the launch traced here: 714 us
  blocking collectives  344 us (48%)
  local copies, waits for them, and re-layouts  148 us (20%)
  waiting for transfers between devices  66.8 us (9%)
  matrix products  55.2 us (8%)
  other arithmetic  39.6 us (5%)
  loops' own time  37.5 us (5%)
  starting transfers between devices  21.5 us (3%)
    all_gather x1, blocking collectives, shards(): stats_all = lax.all_gather(stat_wide, 'span', axis=0, tiled=True)  177 us
    all_to_all x1, blocking collectives, shards(): jax.lax.all_to_all(jnp.stack([local_values for _ in range(jax.lax.axis_si...  166 us
    ppermute x4, waiting for transfers between devices, padded(): lax.ppermute(lax.slice_in_dim(block, block.shape[dim] - width, None, axis...  55.6 us
    another operation x3, loops' own time, over_tiles(): result, _ = lax.scan(inner, carried, (piece, block_ids))  31.1 us
    unnamed x34, local copies, waits for them, and re-layouts  26.6 us
    dot_general x8, matrix products, key_run(): jnp.einsum('hqk,qhd->khd', slope, asking, preferred_element_type=jnp.floa...  20.7 us
    squeeze x10, local copies, waits for them, and re-layouts, over_tiles(): result, _ = lax.scan(inner, carried, (piece, block_ids))  19.7 us
    dynamic_slice x24, local copies, waits for them, and re-layouts, over_tiles(): result, _ = lax.scan(inner, carried, (piece, block_ids))  19.4 us
  transfers between devices with their start and end apart: 8, of which 5 were waited for; matrix products, arithmetic and copies ran while one was open for 8% of the time, Pallas kernels for 0%

profile of v1, /device:TPU:2, one launch (start us, length us, event | category | flops | bytes accessed | tf_op | source)
XLA Modules:
  0.0 713.6 jit_solution(4891781726859204003)
XLA Ops:
  7.6 166.2 %all_to_all.5 = bf16[8,1,3,4,12,3072]{5,3,4,2,1,0:T(4,128)(2,1)S(1)} all-to-all(bf16[8,1,3,4,12,3072]{5,3,4,2,1,0:T(4,128)(2,1)S(1)} %stack.2), channel_id=1, replica_groups=mesh['span'=8,'ha'=8,'wa'=4] {'span'}, dimensions={0} | all-to-all | bytes 14155776 | tf_op jit(solution)/shard_map/all_to_all | solution.py:185
  173.8 5.0 fusion.57
  190.6 33.0 %collective-permute-done = bf16[8,3,2,12,3072]{4,0,3,2,1:T(8,128)(2,1)S(1)} collective-permute-done((bf16[8,3,2,12,3072]{4,0,3,2,1:T(8,128)(2,1)S(1)}, bf16[8,3,2,12,3072]{4,0,3,2,1:T(8,128)(2,1)S(1)}, u32[]{:S(2)}, u32[]{:S(2)}) %collective-permute-start) | collective-permute-done | bytes 3538976 | tf_op jit(solution)/shard_map/ppermute | solution.py:15
  229.4 5.6 copy.82
  235.1 5.3 pad_maximum_fusion.3
  240.4 4.9 collective-permute-start.2
  272.3 22.7 %collective-permute-done.2 = bf16[8,3,8,2,3072]{4,2,3,1,0:T(8,128)(2,1)} collective-permute-done((bf16[8,3,8,2,3072]{4,2,3,1,0:T(8,128)(2,1)}, bf16[8,3,8,2,3072]{4,2,3,1,0:T(8,128)(2,1)}, u32[]{:S(2)}, u32[]{:S(2)}) %collective-permute-start.2) | collective-permute-done | bytes 2359328 | tf_op jit(solution)/shard_map/ppermute | solution.py:15
  295.0 6.1 collective-permute-done.3
  301.1 13.9 %pad_maximum_fusion = bf16[8,3,8,16,3072]{4,2,3,1,0:T(8,128)(2,1)S(1)} fusion(bf16[8,3,8,2,3072]{4,2,3,1,0:T(8,128)(2,1)} %collective-permute-done.3, bf16[8,3,2,12,3072]{4,2,3,1,0:T(2,128)(2,1)} %copy-done.1, bf16[8,3,4,12,3072]{4,2,3,1,0:T(4,128)(2,1)} %bitcast.96, bf16[8,3,2,12,3072]{4,2,3,1,0:T(2,128)(2,1)S(1)} %copy.81, ...), kind=kLoop, calls=%fused_computation.67 | loop fusion | flops 94371840 | bytes 37748736 | tf_op jit(solution)/shard_map/concatenate | solution.py:19
  315.0 12.6 %copy.84 = bf16[8,3,8,16,3072]{4,3,2,1,0:T(8,128)(2,1)} copy(bf16[8,3,8,16,3072]{4,2,3,1,0:T(8,128)(2,1)S(1)} %pad_maximum_fusion) | data formatting | bytes 37748736
  327.7 26.6 %while.42 = (s32[]{:T(128)}, f32[6,144]{1,0:T(8,128)S(1)}, f32[6,144]{1,0:T(8,128)S(1)}, f32[6,144,128]{2,1,0:T(8,128)S(1)}, s32[8]{0:T(128)S(1)}, /*index=5*/s3...) while((s32[]{:T(128)}, f32[6,144]{1,0:T(8,128)S(1)}, ...), condition=%wide.region_6.7_spmd.clone, body=%wide.region_0.6_spmd.clone.sunk | while | flops 172599008 | bytes 17480200 | solution.py:60
  329.6 11.2 %conditional.9 = ((f32[6,144]{1,0:T(8,128)S(1)}, f32[6,144]{1,0:T(8,128)S(1)}, f32[6,144,128]{2,1,0:T(8,128)S(1)})) conditional(s32[]{:T(128)} %convert_element_type.76, (f32[6,144]{1,0:T(8,128)S(1)}, f32[6,144]{1,0:T(8,128)S(1)}, f32[6,144,128]{2,1,0:T(8,128)S(1)}) %tuple.115, (s32[4,12,8,16]{3,2,1,0:T(8,128)S(1)}, s32[]{:T(128)}, s32[8]{0:T(128)}, ...), branch_computations={%region_1.1_spmd, %region_2.0_spmd} | conditional | flops 172599008 | bytes 17479918 | solution.py:120
  364.4 31.3 %while.43 = (s32[]{:T(128)}, f32[6,144,128]{2,1,0:T(8,128)}, s32[8]{0:T(128)}, s32[]{:T(128)}, s32[8]{0:T(128)}, /*index=5*/bf16[8,3,8,16,3072]{4,3,2,1,0:T(8,12...) while((s32[]{:T(128)}, f32[6,144,128]{2,1,0:T(8,128)}, ...), condition=%wide.region_11.12_spmd.clone, body=%wide.region_7.11_spmd.clone.sunk | while | flops 257089568 | bytes 18095392 | solution.py:60
  366.9 11.0 %conditional.10 = (f32[6,144,128]{2,1,0:T(8,128)}) conditional(s32[]{:T(128)} %convert_element_type.77, f32[6,144,128]{2,1,0:T(8,128)} %get-tuple-element.945, (s32[4,12,8,16]{3,2,1,0:T(8,128)S(1)}, s32[]{:T(128)}, s32[8]{0:T(128)}, bf16[8,3,8,16,3072]{4,3,2,1,0:T(8,128)(2,1)}, s32[]{:T(128)}, /*index=5*/bf16[144,6,128]{2,0,1:T(8,128)(2,1)}, ...), branch_computations={%region_8.8_spmd, %region_9.10_spmd} | conditional | flops 257089568 | bytes 18095118 | solution.py:142
  407.4 177.5 %all_gather.3 = f32[8,3,8,16,12]{3,2,4,1,0:T(8,128)S(1)} all-gather(f32[1,3,8,16,12]{3,2,4,1,0:T(8,128)S(1)} %copy.93), channel_id=1, replica_groups=mesh['span'=8,'ha'=8,'wa'=4] {'span'}, dimensions={0}, use_global_device_ids=true | all-gather | bytes 165888 | tf_op jit(solution)/shard_map/all_gather | solution.py:202
  586.9 123.1 %while.44 = (s32[]{:T(128)}, f32[144,6,128]{2,0,1:T(8,128)S(1)}, f32[144,6,128]{2,0,1:T(8,128)}, s32[8]{0:T(128)S(1)}, s32[]{:T(128)}, /*index=5*/bf16[8,3,8,16,...) while((s32[]{:T(128)}, f32[144,6,128]{2,0,1:T(8,128)S(1)}, ...), condition=%wide.region_16.17_spmd.clone, body=%wide.region_13.16_spmd.clone.sunk | while | flops 342282240 | bytes 23095652 | solution.py:60
  588.8 13.5 %conditional.11 = ((f32[144,6,128]{2,0,1:T(8,128)S(1)}, f32[144,6,128]{2,0,1:T(8,128)})) conditional(s32[]{:T(128)} %convert_element_type.78, (f32[144,6,128]{2,0,1:T(8,128)S(1)}, f32[144,6,128]{2,0,1:T(8,128)}) %tuple.120, (bf16[8,3,8,16,3072]{4,3,2,1,0:T(8,128)(2,1)}, s32[]{:T(128)}, bf16[144,6,128]{2,0,1:T(8,128)(2,1)}, s32[]{:T(128)}, ...), branch_computations={%region_14.14_spmd, %region_15.15_spmd} | conditional | flops 342282240 | bytes 23095408 | solution.py:177
  604.2 13.5 %conditional.11 = ((f32[144,6,128]{2,0,1:T(8,128)S(1)}, f32[144,6,128]{2,0,1:T(8,128)})) conditional(s32[]{:T(128)} %convert_element_type.78, (f32[144,6,128]{2,0,1:T(8,128)S(1)}, f32[144,6,128]{2,0,1:T(8,128)}) %tuple.120, (bf16[8,3,8,16,3072]{4,3,2,1,0:T(8,128)(2,1)}, s32[]{:T(128)}, bf16[144,6,128]{2,0,1:T(8,128)(2,1)}, s32[]{:T(128)}, ...), branch_computations={%region_14.14_spmd, %region_15.15_spmd} | conditional | flops 342282240 | bytes 23095408 | solution.py:177
  619.5 13.5 %conditional.11 = ((f32[144,6,128]{2,0,1:T(8,128)S(1)}, f32[144,6,128]{2,0,1:T(8,128)})) conditional(s32[]{:T(128)} %convert_element_type.78, (f32[144,6,128]{2,0,1:T(8,128)S(1)}, f32[144,6,128]{2,0,1:T(8,128)}) %tuple.120, (bf16[8,3,8,16,3072]{4,3,2,1,0:T(8,128)(2,1)}, s32[]{:T(128)}, bf16[144,6,128]{2,0,1:T(8,128)(2,1)}, s32[]{:T(128)}, ...), branch_computations={%region_14.14_spmd, %region_15.15_spmd} | conditional | flops 342282240 | bytes 23095408 | solution.py:177
  634.9 13.5 %conditional.11 = ((f32[144,6,128]{2,0,1:T(8,128)S(1)}, f32[144,6,128]{2,0,1:T(8,128)})) conditional(s32[]{:T(128)} %convert_element_type.78, (f32[144,6,128]{2,0,1:T(8,128)S(1)}, f32[144,6,128]{2,0,1:T(8,128)}) %tuple.120, (bf16[8,3,8,16,3072]{4,3,2,1,0:T(8,128)(2,1)}, s32[]{:T(128)}, bf16[144,6,128]{2,0,1:T(8,128)(2,1)}, s32[]{:T(128)}, ...), branch_computations={%region_14.14_spmd, %region_15.15_spmd} | conditional | flops 342282240 | bytes 23095408 | solution.py:177
  650.3 13.5 %conditional.11 = ((f32[144,6,128]{2,0,1:T(8,128)S(1)}, f32[144,6,128]{2,0,1:T(8,128)})) conditional(s32[]{:T(128)} %convert_element_type.78, (f32[144,6,128]{2,0,1:T(8,128)S(1)}, f32[144,6,128]{2,0,1:T(8,128)}) %tuple.120, (bf16[8,3,8,16,3072]{4,3,2,1,0:T(8,128)(2,1)}, s32[]{:T(128)}, bf16[144,6,128]{2,0,1:T(8,128)(2,1)}, s32[]{:T(128)}, ...), branch_computations={%region_14.14_spmd, %region_15.15_spmd} | conditional | flops 342282240 | bytes 23095408 | solution.py:177
  665.7 13.5 %conditional.11 = ((f32[144,6,128]{2,0,1:T(8,128)S(1)}, f32[144,6,128]{2,0,1:T(8,128)})) conditional(s32[]{:T(128)} %convert_element_type.78, (f32[144,6,128]{2,0,1:T(8,128)S(1)}, f32[144,6,128]{2,0,1:T(8,128)}) %tuple.120, (bf16[8,3,8,16,3072]{4,3,2,1,0:T(8,128)(2,1)}, s32[]{:T(128)}, bf16[144,6,128]{2,0,1:T(8,128)(2,1)}, s32[]{:T(128)}, ...), branch_computations={%region_14.14_spmd, %region_15.15_spmd} | conditional | flops 342282240 | bytes 23095408 | solution.py:177
  681.1 13.5 %conditional.11 = ((f32[144,6,128]{2,0,1:T(8,128)S(1)}, f32[144,6,128]{2,0,1:T(8,128)})) conditional(s32[]{:T(128)} %convert_element_type.78, (f32[144,6,128]{2,0,1:T(8,128)S(1)}, f32[144,6,128]{2,0,1:T(8,128)}) %tuple.120, (bf16[8,3,8,16,3072]{4,3,2,1,0:T(8,128)(2,1)}, s32[]{:T(128)}, bf16[144,6,128]{2,0,1:T(8,128)(2,1)}, s32[]{:T(128)}, ...), branch_computations={%region_14.14_spmd, %region_15.15_spmd} | conditional | flops 342282240 | bytes 23095408 | solution.py:177
  696.5 13.5 %conditional.11 = ((f32[144,6,128]{2,0,1:T(8,128)S(1)}, f32[144,6,128]{2,0,1:T(8,128)})) conditional(s32[]{:T(128)} %convert_element_type.78, (f32[144,6,128]{2,0,1:T(8,128)S(1)}, f32[144,6,128]{2,0,1:T(8,128)}) %tuple.120, (bf16[8,3,8,16,3072]{4,3,2,1,0:T(8,128)(2,1)}, s32[]{:T(128)}, bf16[144,6,128]{2,0,1:T(8,128)(2,1)}, s32[]{:T(128)}, ...), branch_computations={%region_14.14_spmd, %region_15.15_spmd} | conditional | flops 342282240 | bytes 23095408 | solution.py:177
  (303 shorter events, 222.3 us)
Async XLA Ops:
  173.8 61.3 %copy-start = (bf16[8,1,3,4,12,3072]{5,3,4,2,1,0:T(4,128)(2,1)}, bf16[8,1,3,4,12,3072]{5,3,4,2,1,0:T(4,128)(2,1)S(1)}, u32[]{:S(2)}) copy-start(bf16[8,1,3,4,12,3072]{5,3,4,2,1,0:T(4,128)(2,1)S(1)} %all_to_all.5) | copy-start | bytes 21233668
  180.7 42.8 %collective-permute-start = (bf16[8,3,2,12,3072]{4,0,3,2,1:T(8,128)(2,1)S(1)}, bf16[8,3,2,12,3072]{4,0,3,2,1:T(8,128)(2,1)S(1)}, u32[]{:S(2)}, u32[]{:S(2)}) collective-permute-start(bf16[8,3,2,12,3072]{4,0,3,2,1:T(8,128)(2,1)S(1)} %copy.79), channel_id=1, source_target_pairs={{0,4},{4,8},{8,12},{12,16},{16,20},{20,24},{24,28},{1,5},{5,9},{9,... | collective-permute-start | bytes 10616840 | tf_op jit(solution)/shard_map/ppermute | solution.py:15
  186.4 42.9 %collective-permute-start.1 = (bf16[8,3,2,12,3072]{4,0,3,2,1:T(8,128)(2,1)}, bf16[8,3,2,12,3072]{4,0,3,2,1:T(8,128)(2,1)}, u32[]{:S(2)}, u32[]{:S(2)}) collective-permute-start(bf16[8,3,2,12,3072]{4,0,3,2,1:T(8,128)(2,1)} %copy.80), channel_id=1, source_target_pairs={{4,0},{8,4},{12,8},{16,12},{20,16},{24,20},{28,24},{5,1},{9,5},{13... | collective-permute-start | bytes 10616840 | tf_op jit(solution)/shard_map/ppermute | solution.py:18
  235.0 5.3 copy-start.1
  235.0 11.7 %copy-start.6 = (bf16[1,3,4,12,768]{4,2,3,1,0:T(4,128)(2,1)S(1)}, bf16[1,3,4,12,768]{4,2,3,1,0:T(4,128)(2,1)}, u32[]{:S(2)}) copy-start(bf16[1,3,4,12,768]{4,2,3,1,0:T(4,128)(2,1)} %param.18) | copy-start | bytes 663556
  235.1 12.4 %copy-start.7 = (bf16[1,3,4,12,768]{4,2,3,1,0:T(4,128)(2,1)S(1)}, bf16[1,3,4,12,768]{4,2,3,1,0:T(4,128)(2,1)}, u32[]{:S(2)}) copy-start(bf16[1,3,4,12,768]{4,2,3,1,0:T(4,128)(2,1)} %param.21) | copy-start | bytes 663556
  235.1 13.2 %copy-start.8 = (bf16[1,3,4,12,768]{4,2,3,1,0:T(4,128)(2,1)S(1)}, bf16[1,3,4,12,768]{4,2,3,1,0:T(4,128)(2,1)}, u32[]{:S(2)}) copy-start(bf16[1,3,4,12,768]{4,2,3,1,0:T(4,128)(2,1)} %param.19) | copy-start | bytes 663556
  235.1 13.9 %copy-start.9 = (bf16[1,3,4,12,768]{4,2,3,1,0:T(4,128)(2,1)S(1)}, bf16[1,3,4,12,768]{4,2,3,1,0:T(4,128)(2,1)}, u32[]{:S(2)}) copy-start(bf16[1,3,4,12,768]{4,2,3,1,0:T(4,128)(2,1)} %param.20) | copy-start | bytes 663556
  240.4 54.6 %collective-permute-start.2 = (bf16[8,3,8,2,3072]{4,2,3,1,0:T(8,128)(2,1)}, bf16[8,3,8,2,3072]{4,2,3,1,0:T(8,128)(2,1)}, u32[]{:S(2)}, u32[]{:S(2)}) collective-permute-start(bf16[8,3,8,2,3072]{4,2,3,1,0:T(8,128)(2,1)} %get-tuple-element.644), channel_id=1, source_target_pairs={{0,1},{1,2},{2,3},{4,5},{5,6},{6,7},{8,9},{9,10},{10,11},{12,13},{... | collective-permute-start | bytes 7077896 | tf_op jit(solution)/shard_map/ppermute | solution.py:15
  245.3 55.8 %collective-permute-start.3 = (bf16[8,3,8,2,3072]{4,2,3,1,0:T(8,128)(2,1)}, bf16[8,3,8,2,3072]{4,2,3,1,0:T(8,128)(2,1)}, u32[]{:S(2)}, u32[]{:S(2)}) collective-permute-start(bf16[8,3,8,2,3072]{4,2,3,1,0:T(8,128)(2,1)} %get-tuple-element.645), channel_id=1, source_target_pairs={{1,0},{2,1},{3,2},{5,4},{6,5},{7,6},{9,8},{10,9},{11,10},{13,12},{... | collective-permute-start | bytes 7077896 | tf_op jit(solution)/shard_map/ppermute | solution.py:18
  249.7 21.0 %copy-start.12 = (s32[6]{0:T(128)S(1)}, s32[6]{0:T(128)}, u32[]{:S(2)}) copy-start(s32[6]{0:T(128)} %param.22) | copy-start | bytes 76
  257.4 10.6 %copy-start.13 = (pred[128]{0:T(512)(128)(4,1)S(1)}, pred[128]{0:T(512)(128)(4,1)}, u32[]{:S(2)}) copy-start(pred[128]{0:T(512)(128)(4,1)} %and.135) | copy-start | bytes 388
  315.0 12.7 %copy-start.2 = (s32[4,12,8,16]{3,2,1,0:T(8,128)S(1)}, s32[4,12,8,16]{3,2,1,0:T(8,128)}, u32[]{:S(2)}) copy-start(s32[4,12,8,16]{3,2,1,0:T(8,128)} %broadcast_maximum_fusion) | copy-start | bytes 73732
  357.3 38.4 %collective-permute-start.4 = (f32[1,3,2,12,12]{3,2,1,4,0:T(2,128)}, f32[1,3,2,12,12]{3,2,1,4,0:T(2,128)}, u32[]{:S(2)}, u32[]{:S(2)}) collective-permute-start(f32[1,3,2,12,12]{3,2,1,4,0:T(2,128)} %get-tuple-element.652), channel_id=1, source_target_pairs={{0,4},{4,8},{8,12},{12,16},{16,20},{20,24},{24,28},{1,5},{5,9},{9,... | collective-permute-start | bytes 10376 | tf_op jit(solution)/shard_map/ppermute | solution.py:15
  359.5 36.2 %collective-permute-start.5 = (f32[1,3,2,12,12]{3,2,1,4,0:T(2,128)}, f32[1,3,2,12,12]{3,2,1,4,0:T(2,128)}, u32[]{:S(2)}, u32[]{:S(2)}) collective-permute-start(f32[1,3,2,12,12]{3,2,1,4,0:T(2,128)} %get-tuple-element.653), channel_id=1, source_target_pairs={{4,0},{8,4},{12,8},{16,12},{20,16},{24,20},{28,24},{5,1},{9,5},{13... | collective-permute-start | bytes 10376 | tf_op jit(solution)/shard_map/ppermute | solution.py:18
  370.1 5.1 copy-start.11
  395.7 6.7 copy-start.10
  396.7 6.8 collective-permute-start.6
  398.9 7.5 %collective-permute-start.7 = (f32[1,3,8,2,12]{3,2,1,4,0:T(8,128)S(1)}, f32[1,3,8,2,12]{3,2,1,4,0:T(8,128)S(1)}, u32[]{:S(2)}, u32[]{:S(2)}) collective-permute-start(f32[1,3,8,2,12]{3,2,1,4,0:T(8,128)S(1)} %get-tuple-element.651), channel_id=1, source_target_pairs={{1,0},{2,1},{3,2},{5,4},{6,5},{7,6},{9,8},{10,9},{11,10},{13,12},{... | collective-permute-start | bytes 6920 | tf_op jit(solution)/shard_map/ppermute | solution.py:18
  600.0 2.2 copy-start.4
  615.4 2.2 copy-start.4
  630.8 2.2 copy-start.4
  646.2 2.2 copy-start.4
  707.7 2.2 copy-start.4
  (12 other events, 23.9 us)
